TPU v7x, 32 devices: a whole 2x2x4 slice. The times are simulated.
32 devices in a mesh: mem: 4 (over y, x), tile: 4 (over z), grp: 2 (over core).
Axes of the slice: x: 2, y: 2, z: 4, core: 2. Of those that a mesh axis runs over, the one named last changes fastest.
Arguments:
- members: float32 [3, 128, 64, 512], P(None, 'mem', ('tile', 'grp')), may hold values from -0.6 to 0.6
- obs_cells: int32 [8, 4, 1024], P(('tile', 'grp'), 'mem'), may hold values from 0 to 1023
- obs_count: int32 [8, 4], P(('tile', 'grp'), 'mem'), may hold values from 128 to 1024, as said below
- obs_values: float32 [8, 4, 1024], P(('tile', 'grp'), 'mem'), may hold values from -0.6 to 0.6
- obs_error: float32 [8, 4, 1024], P(('tile', 'grp'), 'mem'), may hold values from 0.03 to 0.3
- obs_noise: float32 [8, 4, 1024, 128], P(('tile', 'grp'), 'mem'), may hold values from -6 to 6
Outputs:
- analysis: bfloat16 [3, 128, 64, 512], P(None, None, ('tile', 'grp'), 'mem')
Inputs may be any that keep to these rules, and one draw needn't show every extreme that they name: `obs_count`: a multiple of 128; some tile has exactly 1024 live slots in every draw.
All inputs are finite; a program needn't handle non-finite values.
Results may differ from a plain program's by a relative error of at most 0.0058.
Values may be sent and summed in bfloat16 or wider, within the bound.
A program may use at most 64 MiB of HBM per device.

v0:
```python
import jax
import jax.numpy as jnp
from jax import lax
from jax.sharding import PartitionSpec as P

STEPS = 4


courant = 0.3
gravity = 1.0
coriolis = 0.1


def with_halo(block, sides, width):
    for axis, dim in sides:
        count = lax.axis_size(axis)
        forward = [(i, i + 1) for i in range(count - 1)]
        forward.append((count - 1, 0))
        backward = [(target, source) for source, target in forward]
        low = lax.ppermute(
            lax.slice_in_dim(block, block.shape[dim] - width, None, axis=dim), axis, forward
        )
        high = lax.ppermute(lax.slice_in_dim(block, 0, width, axis=dim), axis, backward)
        block = jnp.concatenate([low, block, high], axis=dim)
    return block


def beside_all(field_e, field_w, field_n, field_s):
    return 0.25 * (field_e + field_w + field_n + field_s)


def advance(padded):
    height = padded[0]
    zonal = padded[1]
    meridional = padded[2]
    height_e, height_w, height_mid = (height[:, 2:, :], height[:, :-2, :], height[:, 1:-1, :])
    zonal_e, zonal_w, zonal_mid = (zonal[:, 2:, :], zonal[:, :-2, :], zonal[:, 1:-1, :])
    merid_e, merid_w, merid_mid = (
        meridional[:, 2:, :],
        meridional[:, :-2, :],
        meridional[:, 1:-1, :],
    )
    height_n, height_s = (jnp.roll(height_mid, -1, axis=2), jnp.roll(height_mid, 1, axis=2))
    zonal_n, zonal_s = (jnp.roll(zonal_mid, -1, axis=2), jnp.roll(zonal_mid, 1, axis=2))
    merid_n, merid_s = (jnp.roll(merid_mid, -1, axis=2), jnp.roll(merid_mid, 1, axis=2))
    new_height = (
        beside_all(height_e, height_w, height_n, height_s)
        - courant * ((1.0 + height_e) * zonal_e - (1.0 + height_w) * zonal_w)
        - courant * ((1.0 + height_n) * merid_n - (1.0 + height_s) * merid_s)
    )
    new_zonal = (
        beside_all(zonal_e, zonal_w, zonal_n, zonal_s)
        - courant
        * (
            0.5 * zonal_e * zonal_e
            + gravity * height_e
            - (0.5 * zonal_w * zonal_w + gravity * height_w)
        )
        - courant * merid_mid * (zonal_n - zonal_s)
        + coriolis * merid_mid
    )
    new_merid = (
        beside_all(merid_e, merid_w, merid_n, merid_s)
        - courant
        * (
            0.5 * merid_n * merid_n
            + gravity * height_n
            - (0.5 * merid_s * merid_s + gravity * height_s)
        )
        - courant * zonal_mid * (merid_e - merid_w)
        - coriolis * zonal_mid
    )
    return jnp.stack([new_height, new_zonal, new_merid])


def body(members, obs_cells, obs_count, obs_values, obs_error, obs_noise):
    fluid_condition = members
    for step_index in range(STEPS):
        padded = with_halo(fluid_condition, ((("tile", "grp"), 2),), 1)
        fluid_condition = advance(padded)
    predict_realizations = fluid_condition.astype(jnp.bfloat16)
    condition_patches = lax.all_to_all(
        predict_realizations, "mem", split_axis=3, concat_axis=1, tiled=True
    )
    ens_size = condition_patches.shape[1]
    tile_rows = condition_patches.shape[2]
    tile_cols = condition_patches.shape[3]
    states = condition_patches.reshape(3, ens_size, tile_rows * tile_cols).astype(jnp.float32)
    cell_ids = obs_cells[0, 0]
    live_count = obs_count[0, 0]
    obs_vals = obs_values[0, 0]
    obs_std = obs_error[0, 0]
    perturb = obs_noise[0, 0]
    spread = states - jnp.mean(states, axis=1, keepdims=True)
    observed = jnp.take(states[0], cell_ids, axis=1)
    obs_spread = observed - jnp.mean(observed, axis=0, keepdims=True)
    slot_ids = jnp.arange(obs_vals.shape[0], dtype=jnp.int32)
    weights = jnp.where(slot_ids < live_count, 1.0 / (obs_std * obs_std), 0.0)
    weighted = obs_spread * weights[None, :]
    innov = obs_vals[None, :] + obs_std[None, :] * perturb.T - observed
    identity = (ens_size - 1.0) * jnp.eye(ens_size, dtype=jnp.float32)
    gram = identity + jnp.dot(weighted, obs_spread.T, precision=lax.Precision.HIGHEST)
    rhs_matrix = jnp.dot(weighted, innov.T, precision=lax.Precision.HIGHEST)
    factor = jnp.linalg.cholesky(gram)
    weight_matrix = jax.scipy.linalg.cho_solve((factor, True), rhs_matrix)
    update = jnp.einsum("vkc,kj->vjc", spread, weight_matrix, precision=lax.Precision.HIGHEST)
    result = (states + update).astype(jnp.bfloat16)
    return result.reshape(3, ens_size, tile_rows, tile_cols)


def solution(mesh):
    in_specs = (
        P(None, "mem", ("tile", "grp"), None),
        P(("tile", "grp"), "mem", None),
        P(("tile", "grp"), "mem"),
        P(("tile", "grp"), "mem", None),
        P(("tile", "grp"), "mem", None),
        P(("tile", "grp"), "mem", None, None),
    )
    out_specs = P(None, None, ("tile", "grp"), "mem")
    return jax.shard_map(body, mesh=mesh, in_specs=in_specs, out_specs=out_specs, check_vma=False)
```

profile of v0, /device:TPU:0, one launch (start us, length us, event | category | flops | bytes accessed | tf_op | source)
XLA Modules:
  0.0 116.6 jit_solution(8921665468865927529)
XLA Ops:
  0.0 2.5 %fusion.102 = (f32[3,32,1,512]{3,2,1,0:T(1,128)S(1)}, f32[3,32,1,512]{3,2,1,0:T(1,128)S(1)}) fusion(f32[3,32,8,512]{3,2,1,0:T(8,128)} %param.6), kind=kLoop, calls=%fused_computation.194 | loop fusion | bytes 786432 | tf_op jit(solution)/shard_map/slice | solution.py:23
  3.1 4.1 %collective-permute-start.1 = (f32[3,32,1,512]{3,1,2,0:T(8,128)S(1)}, f32[3,32,1,512]{3,1,2,0:T(8,128)S(1)}, u32[]{:S(2)}, u32[]{:S(2)}) collective-permute-start(f32[3,32,1,512]{3,1,2,0:T(8,128)S(1)} %copy.504), channel_id=1, source_target_pairs={{1,0},{2,1},{3,2},{4,3},{5,4},{6,5},{7,6},{0,7},{9,8},{10,9},{11,1... | collective-permute-start | bytes 589832 | tf_op jit(solution)/shard_map/ppermute | solution.py:23
  7.2 3.4 %collective-permute-done = f32[3,32,1,512]{3,1,2,0:T(8,128)S(1)} collective-permute-done((f32[3,32,1,512]{3,1,2,0:T(8,128)S(1)}, f32[3,32,1,512]{3,1,2,0:T(8,128)S(1)}, u32[]{:S(2)}, u32[]{:S(2)}) %collective-permute-start) | collective-permute-done | bytes 196640 | tf_op jit(solution)/shard_map/ppermute | solution.py:20
  10.6 0.9 constant_dynamic-update-slice_fusion.1
  14.2 0.9 collective-permute-start.2
  15.2 2.7 %collective-permute-start.3 = (f32[3,32,1,512]{3,1,2,0:T(8,128)S(1)}, f32[3,32,1,512]{3,1,2,0:T(8,128)S(1)}, u32[]{:S(2)}, u32[]{:S(2)}) collective-permute-start(f32[3,32,1,512]{3,1,2,0:T(8,128)S(1)} %get-tuple-element.22), channel_id=1, source_target_pairs={{1,0},{2,1},{3,2},{4,3},{5,4},{6,5},{7,6},{0,7},{9,8},{10,9},{11,1... | collective-permute-start | bytes 589832 | tf_op jit(solution)/shard_map/ppermute | solution.py:23
  17.8 3.5 %collective-permute-done.2 = f32[3,32,1,512]{3,1,2,0:T(8,128)S(1)} collective-permute-done((f32[3,32,1,512]{3,1,2,0:T(8,128)S(1)}, f32[3,32,1,512]{3,1,2,0:T(8,128)S(1)}, u32[]{:S(2)}, u32[]{:S(2)}) %collective-permute-start.2) | collective-permute-done | bytes 196640 | tf_op jit(solution)/shard_map/ppermute | solution.py:20
  24.4 1.2 %collective-permute-start.4 = (f32[3,32,1,512]{3,1,2,0:T(8,128)S(1)}, f32[3,32,1,512]{3,1,2,0:T(8,128)S(1)}, u32[]{:S(2)}, u32[]{:S(2)}) collective-permute-start(f32[3,32,1,512]{3,1,2,0:T(8,128)S(1)} %get-tuple-element.19), channel_id=1, source_target_pairs={{0,1},{1,2},{2,3},{3,4},{4,5},{5,6},{6,7},{7,0},{8,9},{9,10},{10,1... | collective-permute-start | bytes 589832 | tf_op jit(solution)/shard_map/ppermute | solution.py:20
  25.6 2.5 %collective-permute-start.5 = (f32[3,32,1,512]{3,1,2,0:T(8,128)S(1)}, f32[3,32,1,512]{3,1,2,0:T(8,128)S(1)}, u32[]{:S(2)}, u32[]{:S(2)}) collective-permute-start(f32[3,32,1,512]{3,1,2,0:T(8,128)S(1)} %get-tuple-element.20), channel_id=1, source_target_pairs={{1,0},{2,1},{3,2},{4,3},{5,4},{6,5},{7,6},{0,7},{9,8},{10,9},{11,1... | collective-permute-start | bytes 589832 | tf_op jit(solution)/shard_map/ppermute | solution.py:23
  28.7 2.7 %collective-permute-done.4 = f32[3,32,1,512]{3,1,2,0:T(8,128)S(1)} collective-permute-done((f32[3,32,1,512]{3,1,2,0:T(8,128)S(1)}, f32[3,32,1,512]{3,1,2,0:T(8,128)S(1)}, u32[]{:S(2)}, u32[]{:S(2)}) %collective-permute-start.4) | collective-permute-done | bytes 196640 | tf_op jit(solution)/shard_map/ppermute | solution.py:20
  34.5 1.4 %collective-permute-start.6 = (f32[3,32,1,512]{3,1,2,0:T(8,128)S(1)}, f32[3,32,1,512]{3,1,2,0:T(8,128)S(1)}, u32[]{:S(2)}, u32[]{:S(2)}) collective-permute-start(f32[3,32,1,512]{3,1,2,0:T(8,128)S(1)} %get-tuple-element.17), channel_id=1, source_target_pairs={{0,1},{1,2},{2,3},{3,4},{4,5},{5,6},{6,7},{7,0},{8,9},{9,10},{10,1... | collective-permute-start | bytes 589832 | tf_op jit(solution)/shard_map/ppermute | solution.py:20
  36.0 2.4 %collective-permute-start.7 = (f32[3,32,1,512]{3,1,2,0:T(8,128)S(1)}, f32[3,32,1,512]{3,1,2,0:T(8,128)S(1)}, u32[]{:S(2)}, u32[]{:S(2)}) collective-permute-start(f32[3,32,1,512]{3,1,2,0:T(8,128)S(1)} %get-tuple-element.18), channel_id=1, source_target_pairs={{1,0},{2,1},{3,2},{4,3},{5,4},{6,5},{7,6},{0,7},{9,8},{10,9},{11,1... | collective-permute-start | bytes 589832 | tf_op jit(solution)/shard_map/ppermute | solution.py:23
  38.4 3.2 %collective-permute-done.6 = f32[3,32,1,512]{3,1,2,0:T(8,128)S(1)} collective-permute-done((f32[3,32,1,512]{3,1,2,0:T(8,128)S(1)}, f32[3,32,1,512]{3,1,2,0:T(8,128)S(1)}, u32[]{:S(2)}, u32[]{:S(2)}) %collective-permute-start.6) | collective-permute-done | bytes 196640 | tf_op jit(solution)/shard_map/ppermute | solution.py:20
  44.7 1.0 pad_maximum_fusion.3
  45.7 3.7 %copy.488 = bf16[3,32,8,512]{1,2,0,3:T(8,128)(2,1)S(1)} copy(bf16[3,32,8,512]{3,1,2,0:T(8,128)(2,1)} %pad_maximum_fusion.3) | data formatting | bytes 1572864 | tf_op jit(solution)/shard_map/stack | solution.py:73
  49.4 3.8 %reshape.97 = bf16[4,2,49152]{2,1,0:T(2,128)(2,1)} reshape(bf16[512,3,8,32]{3,2,1,0:T(8,128)(2,1)S(1)} %bitcast.109) | data formatting | bytes 1572864
  53.2 8.5 %all-to-all-start = ((bf16[4,2,49152]{2,1,0:T(2,128)(2,1)}), bf16[4,2,49152]{2,1,0:T(2,128)(2,1)}, u32[]{:S(2)}, u32[]{:S(2)}) async-start(bf16[4,2,49152]{2,1,0:T(2,128)(2,1)} %reshape.97), calls=%async_computation | async-start | bytes 1572864 | tf_op jit(solution)/shard_map/all_to_all | solution.py:82
  61.8 8.8 %all-to-all-done = bf16[4,2,49152]{2,1,0:T(2,128)(2,1)} async-done(((bf16[4,2,49152]{2,1,0:T(2,128)(2,1)}), bf16[4,2,49152]{2,1,0:T(2,128)(2,1)}, u32[]{:S(2)}, u32[]{:S(2)}) %all-to-all-start) | async-done | bytes 786464 | tf_op jit(solution)/shard_map/all_to_all | solution.py:82
  70.5 3.2 %reshape.98 = bf16[512,3,8,32]{3,2,1,0:T(8,128)(2,1)S(1)} reshape(bf16[4,2,49152]{2,1,0:T(2,128)(2,1)} %all-to-all-done) | data formatting | bytes 1572864
  73.8 3.2 %convert_reduce_fusion = f32[3,8,512]{1,0,2:T(4,128)} fusion(bf16[512,3,8,32]{3,2,1,0:T(8,128)(2,1)S(1)} %reshape.98), kind=kLoop, calls=%fused_computation.6 | loop fusion | flops 774144 | bytes 835584 | tf_op jit(solution)/shard_map/reduce_sum | solution.py:94
  76.9 3.0 %copy.489 = f32[3,32,8,4,128]{4,2,1,3,0:T(8,128)} copy(bf16[3,32,8,4,128]{1,2,0,4,3:T(8,128)(2,1)S(1)} %bitcast.108) | data formatting | bytes 2359296 | tf_op jit(solution)/shard_map/convert_element_type | solution.py:88
  79.9 1.2 slice.575
  81.1 1.5 %convert_element_type.25 = f32[3,128,1024]{2,1,0:T(8,128)S(1)} reshape(f32[3,4,32,8,128]{4,3,2,1,0:T(8,128)} %bitcast.111) | data formatting | bytes 3145728 | tf_op jit(solution)/shard_map/convert_element_type | solution.py:88
  83.4 3.0 %gather_fusion = f32[1024,128]{1,0:T(8,128)S(1)} fusion(f32[128,1024]{0,1:T(8,128)S(1)} %copy.490, s32[1024]{0:T(1024)S(1)} %broadcast_clamp_fusion), kind=kCustom, calls=%fused_computation | custom fusion | bytes 1052672 | tf_op jit(solution)/shard_map/jit(_take)/gather | solution.py:95
  86.9 1.8 %fusion.6 = f32[128,128]{1,0:T(8,128)S(1)} fusion(f32[1024,128]{1,0:T(8,128)S(1)} %gather_fusion, f32[1024]{0:T(1024)S(1)} %divide_select_fusion, f32[1024]{0:T(1024)S(1)} %broadcast_multiply_fusion, pred[1024]{0:T(1024)(128)(4,1)S(1)} %compare_and_fusion), kind=kOutput, calls=%fused_computation.28 | convolution fusion | flops 201981952 | bytes 599040 | tf_op jit(solution)/shard_map/dot_general | solution.py:102
  88.7 11.7 %cholesky.16 = f32[128,128]{1,0:T(8,128)S(1)} custom-call(f32[128,128]{1,0:T(8,128)S(1)} %fusion.99), custom_call_target="Cholesky" | custom-call | tf_op jit(solution)/shard_map/jit(cholesky)/cholesky | solution.py:104
  100.5 0.6 compare_reduce_fusion
  101.1 0.7 fusion.94
  101.8 9.8 %custom-call.10 = f32[1,128,128]{1,2,0:T(8,128)S(1)} custom-call(f32[1,128,128]{2,1,0:T(8,128)S(1)} %fusion.94), custom_call_target="InvertDiagBlocksLowerTriangular" | custom-call | tf_op jit(solution)/shard_map/jit(_cho_solve)/triangular_solve | solution.py:105
  111.6 1.9 %fusion.8 = f32[128,128]{1,0:T(8,128)S(1)} fusion(f32[1,1,1024,128]{3,2,1,0:T(8,128)S(1)} %copy-done.2, f32[1024,128]{1,0:T(8,128)S(1)} %gather_fusion, f32[1024]{0:T(1024)S(1)} %divide_select_fusion, f32[1024]{0:T(1024)S(1)} %broadcast_multiply_fusion, f32[1024]{0:T(1024)S(1)} %bitcast.118, f32[1024]{0:T(1024)S(1)} %bitcast.121, ...), kind=kOutput, calls=%fused_computation.30 | convolution fusion | flops 202244096 | bytes 1131520 | tf_op jit(solution)/shard_map/dot_general | solution.py:103
  114.1 1.4 %fusion = bf16[3,128,1024]{2,1,0:T(8,128)(2,1)S(1)} fusion(f32[3,128,1024]{2,1,0:T(8,128)S(1)} %convert_element_type.25, f32[128,128,1]{0,1,2:T(8,128)S(1)} %convolution_bitcast_fusion, f32[3,1024]{1,0:T(4,128)S(1)} %bitcast.116), kind=kOutput, calls=%fused_computation.5 | convolution fusion | flops 605159424 | bytes 2437120 | tf_op jit(solution)/shard_map/vkc,kj->vjc/dot_general | solution.py:106
  115.6 1.1 copy.499
  (82 shorter events, 14.2 us)
Async XLA Ops:
  0.0 10.5 %copy-start.1 = (f32[3,32,8,512]{3,2,1,0:T(8,128)S(1)}, f32[3,32,8,512]{3,2,1,0:T(8,128)}, u32[]{:S(2)}) copy-start(f32[3,32,8,512]{3,2,1,0:T(8,128)} %param.6) | copy-start | bytes 4718596
  2.5 8.0 %collective-permute-start = (f32[3,32,1,512]{3,1,2,0:T(8,128)S(1)}, f32[3,32,1,512]{3,1,2,0:T(8,128)S(1)}, u32[]{:S(2)}, u32[]{:S(2)}) collective-permute-start(f32[3,32,1,512]{3,1,2,0:T(8,128)S(1)} %copy.503), channel_id=1, source_target_pairs={{0,1},{1,2},{2,3},{3,4},{4,5},{5,6},{6,7},{7,0},{8,9},{9,10},{10,1... | collective-permute-start | bytes 589832 | tf_op jit(solution)/shard_map/ppermute | solution.py:20
  3.1 8.4 %collective-permute-start.1 = (f32[3,32,1,512]{3,1,2,0:T(8,128)S(1)}, f32[3,32,1,512]{3,1,2,0:T(8,128)S(1)}, u32[]{:S(2)}, u32[]{:S(2)}) collective-permute-start(f32[3,32,1,512]{3,1,2,0:T(8,128)S(1)} %copy.504), channel_id=1, source_target_pairs={{1,0},{2,1},{3,2},{4,3},{5,4},{6,5},{7,6},{0,7},{9,8},{10,9},{11,1... | collective-permute-start | bytes 589832 | tf_op jit(solution)/shard_map/ppermute | solution.py:23
  14.2 7.1 %collective-permute-start.2 = (f32[3,32,1,512]{3,1,2,0:T(8,128)S(1)}, f32[3,32,1,512]{3,1,2,0:T(8,128)S(1)}, u32[]{:S(2)}, u32[]{:S(2)}) collective-permute-start(f32[3,32,1,512]{3,1,2,0:T(8,128)S(1)} %get-tuple-element.21), channel_id=1, source_target_pairs={{0,1},{1,2},{2,3},{3,4},{4,5},{5,6},{6,7},{7,0},{8,9},{9,10},{10,1... | collective-permute-start | bytes 589832 | tf_op jit(solution)/shard_map/ppermute | solution.py:20
  15.2 6.1 %collective-permute-start.3 = (f32[3,32,1,512]{3,1,2,0:T(8,128)S(1)}, f32[3,32,1,512]{3,1,2,0:T(8,128)S(1)}, u32[]{:S(2)}, u32[]{:S(2)}) collective-permute-start(f32[3,32,1,512]{3,1,2,0:T(8,128)S(1)} %get-tuple-element.22), channel_id=1, source_target_pairs={{1,0},{2,1},{3,2},{4,3},{5,4},{6,5},{7,6},{0,7},{9,8},{10,9},{11,1... | collective-permute-start | bytes 589832 | tf_op jit(solution)/shard_map/ppermute | solution.py:23
  24.4 7.0 %collective-permute-start.4 = (f32[3,32,1,512]{3,1,2,0:T(8,128)S(1)}, f32[3,32,1,512]{3,1,2,0:T(8,128)S(1)}, u32[]{:S(2)}, u32[]{:S(2)}) collective-permute-start(f32[3,32,1,512]{3,1,2,0:T(8,128)S(1)} %get-tuple-element.19), channel_id=1, source_target_pairs={{0,1},{1,2},{2,3},{3,4},{4,5},{5,6},{6,7},{7,0},{8,9},{9,10},{10,1... | collective-permute-start | bytes 589832 | tf_op jit(solution)/shard_map/ppermute | solution.py:20
  25.6 5.9 %collective-permute-start.5 = (f32[3,32,1,512]{3,1,2,0:T(8,128)S(1)}, f32[3,32,1,512]{3,1,2,0:T(8,128)S(1)}, u32[]{:S(2)}, u32[]{:S(2)}) collective-permute-start(f32[3,32,1,512]{3,1,2,0:T(8,128)S(1)} %get-tuple-element.20), channel_id=1, source_target_pairs={{1,0},{2,1},{3,2},{4,3},{5,4},{6,5},{7,6},{0,7},{9,8},{10,9},{11,1... | collective-permute-start | bytes 589832 | tf_op jit(solution)/shard_map/ppermute | solution.py:23
  34.5 3.9 %copy-start.4 = (s32[1,1,1024]{2,1,0:T(1,128)S(1)}, s32[1,1,1024]{2,1,0:T(1,128)}, u32[]{:S(2)}) copy-start(s32[1,1,1024]{2,1,0:T(1,128)} %param.7) | copy-start | bytes 12292
  34.5 7.1 %collective-permute-start.6 = (f32[3,32,1,512]{3,1,2,0:T(8,128)S(1)}, f32[3,32,1,512]{3,1,2,0:T(8,128)S(1)}, u32[]{:S(2)}, u32[]{:S(2)}) collective-permute-start(f32[3,32,1,512]{3,1,2,0:T(8,128)S(1)} %get-tuple-element.17), channel_id=1, source_target_pairs={{0,1},{1,2},{2,3},{3,4},{4,5},{5,6},{6,7},{7,0},{8,9},{9,10},{10,1... | collective-permute-start | bytes 589832 | tf_op jit(solution)/shard_map/ppermute | solution.py:20
  36.0 5.7 %collective-permute-start.7 = (f32[3,32,1,512]{3,1,2,0:T(8,128)S(1)}, f32[3,32,1,512]{3,1,2,0:T(8,128)S(1)}, u32[]{:S(2)}, u32[]{:S(2)}) collective-permute-start(f32[3,32,1,512]{3,1,2,0:T(8,128)S(1)} %get-tuple-element.18), channel_id=1, source_target_pairs={{1,0},{2,1},{3,2},{4,3},{5,4},{6,5},{7,6},{0,7},{9,8},{10,9},{11,1... | collective-permute-start | bytes 589832 | tf_op jit(solution)/shard_map/ppermute | solution.py:23
  49.4 12.4 %copy-start.3 = (f32[1,1,1024]{2,1,0:T(1,128)S(1)}, f32[1,1,1024]{2,1,0:T(1,128)}, u32[]{:S(2)}) copy-start(f32[1,1,1024]{2,1,0:T(1,128)} %param.10) | copy-start | bytes 12292
  53.2 17.4 %all-to-all-start = ((bf16[4,2,49152]{2,1,0:T(2,128)(2,1)}), bf16[4,2,49152]{2,1,0:T(2,128)(2,1)}, u32[]{:S(2)}, u32[]{:S(2)}) async-start(bf16[4,2,49152]{2,1,0:T(2,128)(2,1)} %reshape.97), calls=%async_computation | async-start | bytes 1572864 | tf_op jit(solution)/shard_map/all_to_all | solution.py:82
  79.9 2.7 %copy-start = (f32[3,8,512]{1,0,2:T(4,128)S(1)}, f32[3,8,512]{1,0,2:T(4,128)}, u32[]{:S(2)}) copy-start(f32[3,8,512]{1,0,2:T(4,128)} %convert_reduce_fusion) | copy-start | bytes 147460
  86.5 25.2 %copy-start.2 = (f32[1,1,1024,128]{3,2,1,0:T(8,128)S(1)}, f32[1,1,1024,128]{3,2,1,0:T(8,128)}, u32[]{:S(2)}) copy-start(f32[1,1,1024,128]{3,2,1,0:T(8,128)} %param.11) | copy-start | bytes 1572868
  86.5 25.2 %copy-start.5 = (f32[1,1,1024]{2,1,0:T(1,128)S(1)}, f32[1,1,1024]{2,1,0:T(1,128)}, u32[]{:S(2)}) copy-start(f32[1,1,1024]{2,1,0:T(1,128)} %param.9) | copy-start | bytes 12292
where the time goes:
time: 117 us
  other arithmetic  34.9 us (30%)
  local copies, waits for them, and re-layouts  29 us (25%)
  starting transfers between devices  24.3 us (21%)
  waiting for transfers between devices  21.5 us (18%)
  matrix products  5.64 us (5%)
  between operations  1.17 us (1%)
    ppermute x4, waiting for transfers between devices, with_halo(): lax.ppermute(lax.slice_in_dim(block, block.shape[dim] - width, None, axis...  12.8 us
    another operation x3, other arithmetic, body(): factor = jnp.linalg.cholesky(gram)  12.4 us
    ppermute x4, starting transfers between devices, with_halo(): lax.ppermute(lax.slice_in_dim(block, 0, width, axis=dim), axis, backward)  11.7 us
    another operation x2, other arithmetic, body(): weight_matrix = jax.scipy.linalg.cho_solve((factor, True), rhs_matrix)  10.5 us
    unnamed x21, local copies, waits for them, and re-layouts  9.18 us
    all_to_all x1, waiting for transfers between devices, body(): lax.all_to_all(predict_realizations, 'mem', split_axis=3, concat_axis=1,...  8.77 us
    all_to_all x1, starting transfers between devices, body(): lax.all_to_all(predict_realizations, 'mem', split_axis=3, concat_axis=1,...  8.54 us
    another operation x13, other arithmetic, advance(): return jnp.stack([new_height, new_zonal, new_merid])  7.32 us
  transfers between devices with their start and end apart: 9, of which 5 were waited for; matrix products, arithmetic and copies ran while one was open for 1% of the time, Pallas kernels for 0%

commit v1 on v0

v1 whole, which is shorter than its diff:
```python
import functools

import jax
import jax.numpy as jnp
from jax import lax
from jax.experimental import pallas as pl
from jax.experimental.pallas import tpu as pltpu
from jax.sharding import PartitionSpec as P

STEPS = 4

courant = 0.3
gravity = 1.0
coriolis = 0.1
HIGHEST = lax.Precision.HIGHEST
VMEM_BYTES = 50 * 1024 * 1024


def advance(west, mid, east):
    (hw, uw, vw), (h, u, v), (he, ue, ve) = west, mid, east
    cols = h.shape[1]
    north = lambda q: pltpu.roll(q, cols - 1, 1)
    south = lambda q: pltpu.roll(q, 1, 1)
    hn, hs, un, us, vn, vs = north(h), south(h), north(u), south(u), north(v), south(v)
    new_h = (
        0.25 * (he + hw + hn + hs)
        - courant * ((1.0 + he) * ue - (1.0 + hw) * uw)
        - courant * ((1.0 + hn) * vn - (1.0 + hs) * vs)
    )
    new_u = (
        0.25 * (ue + uw + un + us)
        - courant * ((0.5 * ue * ue + gravity * he) - (0.5 * uw * uw + gravity * hw))
        - courant * v * (un - us)
        + coriolis * v
    )
    new_v = (
        0.25 * (ve + vw + vn + vs)
        - courant * ((0.5 * vn * vn + gravity * hn) - (0.5 * vs * vs + gravity * hs))
        - courant * u * (ve - vw)
        - coriolis * u
    )
    return new_h, new_u, new_v


def forecast_kernel(members, low, high, out, first, second):
    fields, ens, rows, cols = members.shape
    width = low.shape[1]
    parts, tile_cols = out.shape[0], out.shape[4]
    for f in range(fields):
        for r in range(width):
            first[r, f] = low[f, r].astype(jnp.float32)
            first[width + rows + r, f] = high[f, r].astype(jnp.float32)
        for r in range(rows):
            first[width + r, f] = members[f, :, r, :]
    buffers = (first, second)
    for step in range(STEPS):
        src, dst = buffers[step % 2], buffers[(step + 1) % 2]
        start = step + 1
        count = rows + 2 * width - 2 * start
        last = step == STEPS - 1

        def row_step(i, carry, src=src, dst=dst, start=start, last=last):
            row = i + start

            def at(which, m):
                return [src[which, f, pl.ds(m, 8), :] for f in range(fields)]

            for m in range(0, ens, 16):
                done = []
                for half in (m, m + 8):
                    done.append(advance(at(row - 1, half), at(row, half), at(row + 1, half)))
                    if not last:
                        for f in range(fields):
                            dst[row, f, pl.ds(half, 8), :] = done[-1][f]
                if last:
                    for f in range(fields):
                        both = jnp.concatenate([done[0][f], done[1][f]], axis=0)
                        both = both.astype(jnp.bfloat16)
                        for d in range(parts):
                            out[d, f, i, pl.ds(m, 16), :] = both[:, d * tile_cols : (d + 1) * tile_cols]
            return carry

        lax.fori_loop(0, count, row_step, 0)


def eliminate(gram, rhs):
    size = gram.shape[0]
    group = lax.broadcasted_iota(jnp.int32, (8, size), 0)

    def block(_, carry):
        a, b = carry
        for j in range(8):
            row_a, row_b = a[j : j + 1, :], b[j : j + 1, :]
            col = a[:, j : j + 1]
            inverse = 1.0 / a[j : j + 1, j : j + 1]
            row_a, row_b = row_a * inverse, row_b * inverse
            new_a, new_b = a - col * row_a, b - col * row_b
            a = jnp.concatenate([jnp.where(group == j, row_a, new_a[:8]), new_a[8:]], axis=0)
            b = jnp.concatenate([jnp.where(group == j, row_b, new_b[:8]), new_b[8:]], axis=0)
        a = pltpu.roll(jnp.concatenate([a[8:], a[:8]], axis=0), size - 8, 1)
        b = jnp.concatenate([b[8:], b[:8]], axis=0)
        return a, b

    return lax.fori_loop(0, size // 8, block, (gram, rhs))[1]


def analysis_kernel(recv, count, cells, values, error, noise, out, state, tall):
    parts, fields, rows, part_ens, cols = recv.shape
    ens = parts * part_ens
    points = rows * cols
    for s in range(parts):
        for f in range(fields):
            for r in range(rows):
                state[f, s * part_ens : (s + 1) * part_ens, r * cols : (r + 1) * cols] = recv[s, f, r]
    slots = cells.shape[1]
    observed = jnp.zeros((ens, slots), jnp.float32)
    chunk = 256 if points % 256 == 0 else cols
    for c in range(0, points, chunk):
        ids = lax.broadcasted_iota(jnp.int32, (chunk, slots), 0) + c
        pick = jnp.where(ids == cells[...], 1.0, 0.0).astype(jnp.bfloat16)
        observed += jnp.dot(state[0, :, c : c + chunk], pick, preferred_element_type=jnp.float32)
    mean = jnp.sum(observed, axis=0, keepdims=True) * (1.0 / ens)
    spread = observed - mean
    std = error[...]
    slot_ids = lax.broadcasted_iota(jnp.int32, (1, slots), 1)
    weights = jnp.where(slot_ids < count[0, 0], 1.0 / (std * std), 0.0)
    weighted = spread * weights
    gram0 = lax.dot_general(
        weighted, spread, (((1,), (1,)), ((), ())), precision=HIGHEST, preferred_element_type=jnp.float32
    )
    rhs = jnp.dot(weighted * std, noise[...], precision=HIGHEST, preferred_element_type=jnp.float32)
    rhs = rhs + jnp.sum(weighted * (values[...] - mean), axis=1, keepdims=True) - gram0
    eye = jnp.where(
        lax.broadcasted_iota(jnp.int32, (ens, ens), 0) == lax.broadcasted_iota(jnp.int32, (ens, ens), 1), 1.0, 0.0
    )
    solved = eliminate(gram0 + (ens - 1.0) * eye, rhs)
    centred = solved - jnp.sum(solved, axis=0, keepdims=True) * (1.0 / ens) + eye
    turned = centred.T
    upper = turned.astype(jnp.bfloat16)
    lower = (turned - upper.astype(jnp.float32)).astype(jnp.bfloat16)
    for f in range(fields):
        for r in range(rows):
            block = state[f, :, r * cols : (r + 1) * cols]
            tall[:, r, :] = jnp.dot(upper, block, preferred_element_type=jnp.float32) + jnp.dot(
                lower, block, preferred_element_type=jnp.float32
            )
        out[f] = tall[...].astype(jnp.bfloat16)


def vmem():
    return pl.BlockSpec(memory_space=pltpu.VMEM)


def body(members, obs_cells, obs_count, obs_values, obs_error, obs_noise):
    axes = ("tile", "grp")
    count = lax.axis_size(axes)
    forward = [(i, (i + 1) % count) for i in range(count)]
    backward = [(t, s) for s, t in forward]
    fields, ens, rows, cols = members.shape
    parts = lax.axis_size("mem")
    edge = lambda x: jnp.swapaxes(x, 1, 2).astype(jnp.bfloat16)
    low = lax.ppermute(edge(members[:, :, rows - STEPS :, :]), axes, forward)
    high = lax.ppermute(edge(members[:, :, :STEPS, :]), axes, backward)
    tile_cols = cols // parts
    ready = pl.pallas_call(
        forecast_kernel,
        name="forecast",
        out_shape=jax.ShapeDtypeStruct((parts, fields, rows, ens, tile_cols), jnp.bfloat16),
        in_specs=[vmem()] * 3,
        out_specs=vmem(),
        scratch_shapes=[pltpu.VMEM((rows + 2 * STEPS, fields, ens, cols), jnp.float32)] * 2,
        compiler_params=pltpu.CompilerParams(vmem_limit_bytes=VMEM_BYTES),
    )(members, low, high)
    recv = lax.all_to_all(ready, "mem", split_axis=0, concat_axis=0)
    full = ens * parts
    return pl.pallas_call(
        analysis_kernel,
        name="analysis",
        out_shape=jax.ShapeDtypeStruct((fields, full, rows, tile_cols), jnp.bfloat16),
        in_specs=[vmem(), pl.BlockSpec(memory_space=pltpu.SMEM)] + [vmem()] * 4,
        out_specs=vmem(),
        scratch_shapes=[
            pltpu.VMEM((fields, full, rows * tile_cols), jnp.bfloat16),
            pltpu.VMEM((full, rows, tile_cols), jnp.float32),
        ],
        compiler_params=pltpu.CompilerParams(vmem_limit_bytes=VMEM_BYTES),
    )(recv, obs_count, obs_cells[0], obs_values[0], obs_error[0], obs_noise[0, 0])


def solution(mesh):
    in_specs = (
        P(None, "mem", ("tile", "grp"), None),
        P(("tile", "grp"), "mem", None),
        P(("tile", "grp"), "mem"),
        P(("tile", "grp"), "mem", None),
        P(("tile", "grp"), "mem", None),
        P(("tile", "grp"), "mem", None, None),
    )
    out_specs = P(None, None, ("tile", "grp"), "mem")
    return jax.shard_map(body, mesh=mesh, in_specs=in_specs, out_specs=out_specs, check_vma=False)
```

time: 117 us -> 56 us (0.48)
  other arithmetic: 34.9 us -> 0 us
  local copies, waits for them, and re-layouts: 29 us -> 2.44 us
  Pallas kernels: 0 us -> 25.3 us
  starting transfers between devices: 24.3 us -> 9.05 us
  matrix products: 5.64 us -> 0 us
  waiting for transfers between devices: 21.5 us -> 18.4 us
    another operation x18 -> x0, other arithmetic: 30.2 us -> none  [the longest x3 12.4 us: body(): factor = jnp.linalg.cholesky(gram)]
    pallas_call x0 -> x2, Pallas kernels: none -> 25.3 us  [the longest x1 16 us: body(): pl.pallas_call(analysis_kernel, name='analysis', out_shape=jax.ShapeDtype...]
    ppermute x8 -> x2, starting transfers between devices: 15.8 us -> 4.64 us  [the longest x1 4.09 us: body(): high = lax.ppermute(edge(members[:, :, :STEPS, :]), axes, backward)]
    slice x24 -> x0, local copies, waits for them, and re-layouts: 7.25 us -> none  [the longest x1 2.47 us: with_halo(): lax.slice_in_dim(block, 0, width, axis=dim)]
    unnamed x21 -> x11, local copies, waits for them, and re-layouts: 9.18 us -> 2.39 us
    ppermute x8 -> x2, waiting for transfers between devices: 12.8 us -> 7.45 us  [the longest x1 7.01 us: body(): low = lax.ppermute(edge(members[:, :, rows - STEPS:, :]), axes, forward)]
    dot_general x3 -> x0, matrix products: 5.07 us -> none  [the longest x1 1.89 us: body(): rhs_matrix = jnp.dot(weighted, innov.T, precision=lax.Precision.HIGHEST)]
    convert_element_type x2 -> x1, local copies, waits for them, and re-layouts: 4.53 us -> 0.06 us  [body(): edge = lambda x: jnp.swapaxes(x, 1, 2).astype(jnp.bfloat16)]
  transfers between devices with their start and end apart: 9 -> 3, of which waited for: 5 -> 3; matrix products, arithmetic and copies ran while one was open for 1% -> 0% of each run, Pallas kernels for 0% -> 0%
where the time goes in v1:
time: 56 us; the launch traced here: 55.8 us
  Pallas kernels  25.3 us (45%)
  waiting for transfers between devices  18.4 us (33%)
  starting transfers between devices  9.05 us (16%)
  local copies, waits for them, and re-layouts  2.44 us (4%)
  between operations  0.68 us (1%)
    pallas_call x1, Pallas kernels, body(): pl.pallas_call(analysis_kernel, name='analysis', out_shape=jax.ShapeDtype...  16 us
    all_to_all x1, waiting for transfers between devices, body(): recv = lax.all_to_all(ready, 'mem', split_axis=0, concat_axis=0)  10.9 us
    pallas_call x1, Pallas kernels, body(): pl.pallas_call(forecast_kernel, name='forecast', out_shape=jax.ShapeDtype...  9.34 us
    ppermute x1, waiting for transfers between devices, body(): low = lax.ppermute(edge(members[:, :, rows - STEPS:, :]), axes, forward)  7.01 us
    all_to_all x1, starting transfers between devices, body(): recv = lax.all_to_all(ready, 'mem', split_axis=0, concat_axis=0)  4.42 us
    ppermute x1, starting transfers between devices, body(): high = lax.ppermute(edge(members[:, :, :STEPS, :]), axes, backward)  4.09 us
    unnamed x11, local copies, waits for them, and re-layouts  2.39 us
  transfers between devices with their start and end apart: 3, of which 3 were waited for; matrix products, arithmetic and copies ran while one was open for 0% of the time, Pallas kernels for 0%

profile of v1, /device:TPU:0, one launch (start us, length us, event | category | flops | bytes accessed | tf_op | source)
XLA Modules:
  0.0 55.8 jit_solution(8634701694476002808)
XLA Ops:
  0.0 0.0 copy-start
  0.0 2.4 %copy.9 = bf16[3,32,8,512]{3,1,2,0:T(8,128)(2,1)S(1)} copy(f32[3,32,8,512]{3,2,1,0:T(8,128)} %members.1) | data formatting | bytes 2359296 | tf_op args[0]
  2.4 0.1 slice_bitcast_fusion
  2.4 0.5 collective-permute-start
  3.0 4.1 %collective-permute-start.1 = (bf16[3,4,32,512]{3,2,1,0:T(8,128)(2,1)S(1)}, bf16[3,4,32,512]{3,2,1,0:T(8,128)(2,1)S(1)}, u32[]{:S(2)}, u32[]{:S(2)}) collective-permute-start(bf16[3,4,32,512]{3,2,1,0:T(8,128)(2,1)S(1)} %get-tuple-element.5), channel_id=1, source_target_pairs={{1,0},{2,1},{3,2},{4,3},{5,4},{6,5},{7,6},{0,7},{9,8},{10,9},{11,1... | collective-permute-start | bytes 1179656 | tf_op jit(solution)/shard_map/ppermute | solution.py:163
  7.1 7.0 %collective-permute-done.low = bf16[3,4,32,512]{3,2,1,0:T(8,128)(2,1)S(1)} collective-permute-done((bf16[3,4,32,512]{3,2,1,0:T(8,128)(2,1)S(1)}, bf16[3,4,32,512]{3,2,1,0:T(8,128)(2,1)S(1)}, u32[]{:S(2)}, u32[]{:S(2)}) %collective-permute-start) | collective-permute-done | bytes 393248 | tf_op jit(solution)/shard_map/ppermute | solution.py:162
  14.1 0.4 collective-permute-done.1.high
  14.5 0.0 copy-done
  14.5 9.3 %forecast.1 = bf16[4,3,8,32,128]{4,3,2,1,0:T(8,128)(2,1)} custom-call(f32[3,32,8,512]{3,2,1,0:T(8,128)S(1)} %copy-done, bf16[3,4,32,512]{3,2,1,0:T(8,128)(2,1)S(1)} %collective-permute-done.low, bf16[3,4,32,512]{3,2,1,0:T(8,128)(2,1)S(1)} %collective-permute-done.1.high), custom_call_target="tpu_custom_call" | custom-call | tf_op jit(solution)/shard_map/forecast/pallas_call | solution.py:165
  23.9 0.0 copy-start.1
  23.9 0.0 copy-start.2
  23.9 0.0 copy-start.3
  23.9 0.0 copy-start.4
  23.9 4.4 %all-to-all-start = ((bf16[4,3,8,32,128]{4,3,2,1,0:T(8,128)(2,1)}), bf16[4,3,8,32,128]{4,3,2,1,0:T(8,128)(2,1)S(1)}, u32[]{:S(2)}, u32[]{:S(2)}) async-start(bf16[4,3,8,32,128]{4,3,2,1,0:T(8,128)(2,1)} %forecast.1), calls=%async_computation | async-start | bytes 1572864 | tf_op jit(solution)/shard_map/all_to_all | solution.py:174
  28.9 10.9 %all-to-all-done.recv = bf16[4,3,8,32,128]{4,3,2,1,0:T(8,128)(2,1)S(1)} async-done(((bf16[4,3,8,32,128]{4,3,2,1,0:T(8,128)(2,1)}), bf16[4,3,8,32,128]{4,3,2,1,0:T(8,128)(2,1)S(1)}, u32[]{:S(2)}, u32[]{:S(2)}) %all-to-all-start) | async-done | bytes 786464 | tf_op jit(solution)/shard_map/all_to_all | solution.py:174
  39.9 0.0 copy-done.1
  39.9 0.0 copy-done.2
  39.9 0.0 copy-done.3
  39.9 0.0 copy-done.4
  39.9 16.0 %analysis.1 = bf16[3,128,8,128]{3,2,1,0:T(8,128)(2,1)} custom-call(bf16[4,3,8,32,128]{4,3,2,1,0:T(8,128)(2,1)S(1)} %all-to-all-done.recv, s32[1,1]{1,0:T(1,128)S(6)} %copy.10.count, s32[1,1024]{1,0:T(1,128)S(1)} %bitcast.9, f32[1,1024]{1,0:T(1,128)S(1)} %bitcast.10, f32[1,1024]{1,0:T(1,128)S(1)} %bitcast.11, f32[1024,128]{1,0:T(8,128)S(1)} %bitcast.8), custom_call_target="tpu_custom_call" | custom-call | tf_op jit(solution)/shard_map/analysis/pallas_call | solution.py:176
Async XLA Ops:
  0.0 14.5 %copy-start = (f32[3,32,8,512]{3,2,1,0:T(8,128)S(1)}, f32[3,32,8,512]{3,2,1,0:T(8,128)}, u32[]{:S(2)}) copy-start(f32[3,32,8,512]{3,2,1,0:T(8,128)} %members.1) | copy-start | bytes 4718596
  2.4 11.6 %collective-permute-start = (bf16[3,4,32,512]{3,2,1,0:T(8,128)(2,1)S(1)}, bf16[3,4,32,512]{3,2,1,0:T(8,128)(2,1)S(1)}, u32[]{:S(2)}, u32[]{:S(2)}) collective-permute-start(bf16[3,4,32,512]{3,2,1,0:T(8,128)(2,1)S(1)} %get-tuple-element.6), channel_id=1, source_target_pairs={{0,1},{1,2},{2,3},{3,4},{4,5},{5,6},{6,7},{7,0},{8,9},{9,10},{10,1... | collective-permute-start | bytes 1179656 | tf_op jit(solution)/shard_map/ppermute | solution.py:162
  3.0 11.5 %collective-permute-start.1 = (bf16[3,4,32,512]{3,2,1,0:T(8,128)(2,1)S(1)}, bf16[3,4,32,512]{3,2,1,0:T(8,128)(2,1)S(1)}, u32[]{:S(2)}, u32[]{:S(2)}) collective-permute-start(bf16[3,4,32,512]{3,2,1,0:T(8,128)(2,1)S(1)} %get-tuple-element.5), channel_id=1, source_target_pairs={{1,0},{2,1},{3,2},{4,3},{5,4},{6,5},{7,6},{0,7},{9,8},{10,9},{11,1... | collective-permute-start | bytes 1179656 | tf_op jit(solution)/shard_map/ppermute | solution.py:163
  23.9 16.0 %copy-start.1 = (f32[1,1,1024,128]{3,2,1,0:T(8,128)S(1)}, f32[1,1,1024,128]{3,2,1,0:T(8,128)}, u32[]{:S(2)}) copy-start(f32[1,1,1024,128]{3,2,1,0:T(8,128)} %param.11) | copy-start | bytes 1572868
  23.9 16.0 %copy-start.2 = (s32[1,1,1024]{2,1,0:T(1,128)S(1)}, s32[1,1,1024]{2,1,0:T(1,128)}, u32[]{:S(2)}) copy-start(s32[1,1,1024]{2,1,0:T(1,128)} %param.7) | copy-start | bytes 12292
  23.9 16.0 %copy-start.3 = (f32[1,1,1024]{2,1,0:T(1,128)S(1)}, f32[1,1,1024]{2,1,0:T(1,128)}, u32[]{:S(2)}) copy-start(f32[1,1,1024]{2,1,0:T(1,128)} %param.9) | copy-start | bytes 12292
  23.9 16.0 %copy-start.4 = (f32[1,1,1024]{2,1,0:T(1,128)S(1)}, f32[1,1,1024]{2,1,0:T(1,128)}, u32[]{:S(2)}) copy-start(f32[1,1,1024]{2,1,0:T(1,128)} %param.10) | copy-start | bytes 12292
  23.9 16.0 %all-to-all-start = ((bf16[4,3,8,32,128]{4,3,2,1,0:T(8,128)(2,1)}), bf16[4,3,8,32,128]{4,3,2,1,0:T(8,128)(2,1)S(1)}, u32[]{:S(2)}, u32[]{:S(2)}) async-start(bf16[4,3,8,32,128]{4,3,2,1,0:T(8,128)(2,1)} %forecast.1), calls=%async_computation | async-start | bytes 1572864 | tf_op jit(solution)/shard_map/all_to_all | solution.py:174

commit v2 on v1

v2 whole, which is shorter than its diff:
```python
import jax
import jax.numpy as jnp
from jax import lax
from jax.experimental import pallas as pl
from jax.experimental.pallas import tpu as pltpu
from jax.sharding import PartitionSpec as P

STEPS = 4

courant = 0.3
gravity = 1.0
coriolis = 0.1
HIGHEST = lax.Precision.HIGHEST
VMEM_BYTES = 50 * 1024 * 1024


def advance(west, mid, east):
    (hw, uw, vw), (h, u, v), (he, ue, ve) = west, mid, east
    cols = h.shape[1]
    north = lambda q: pltpu.roll(q, cols - 1, 1)
    south = lambda q: pltpu.roll(q, 1, 1)
    hn, hs, un, us, vn, vs = north(h), south(h), north(u), south(u), north(v), south(v)
    new_h = (
        0.25 * (he + hw + hn + hs)
        - courant * ((1.0 + he) * ue - (1.0 + hw) * uw)
        - courant * ((1.0 + hn) * vn - (1.0 + hs) * vs)
    )
    new_u = (
        0.25 * (ue + uw + un + us)
        - courant * ((0.5 * ue * ue + gravity * he) - (0.5 * uw * uw + gravity * hw))
        - courant * v * (un - us)
        + coriolis * v
    )
    new_v = (
        0.25 * (ve + vw + vn + vs)
        - courant * ((0.5 * vn * vn + gravity * hn) - (0.5 * vs * vs + gravity * hs))
        - courant * u * (ve - vw)
        - coriolis * u
    )
    return new_h, new_u, new_v


def eliminate(gram, rhs):
    size = gram.shape[0]
    group = lax.broadcasted_iota(jnp.int32, (8, size), 0)

    def block(_, carry):
        a, b = carry
        for j in range(8):
            row_a, row_b = a[j : j + 1, :], b[j : j + 1, :]
            col = a[:, j : j + 1]
            inverse = 1.0 / a[j : j + 1, j : j + 1]
            row_a, row_b = row_a * inverse, row_b * inverse
            new_a, new_b = a - col * row_a, b - col * row_b
            a = jnp.concatenate([jnp.where(group == j, row_a, new_a[:8]), new_a[8:]], axis=0)
            b = jnp.concatenate([jnp.where(group == j, row_b, new_b[:8]), new_b[8:]], axis=0)
        a = pltpu.roll(jnp.concatenate([a[8:], a[:8]], axis=0), size - 8, 1)
        b = jnp.concatenate([b[8:], b[:8]], axis=0)
        return a, b

    return lax.fori_loop(0, size // 8, block, (gram, rhs))[1]


def neighbour_ids():
    groups = lax.axis_size("grp")
    total = lax.axis_size("tile") * groups
    me = lax.axis_index("tile") * groups + lax.axis_index("grp")
    after, before = lax.rem(me + 1, total), lax.rem(me + total - 1, total)
    return [{"tile": i // groups, "grp": lax.rem(i, groups)} for i in (after, before)]


def kernel(
    members, count, cells, values, error, noise, out,
    first, second, edges, halo, ready, recv, state, pick, tall,
    halo_send, halo_recv, part_send, part_recv,
):
    fields, ens, rows, cols = members.shape
    width = STEPS
    parts, _, _, _, tile_cols = ready.shape
    full = parts * ens
    points = rows * tile_cols
    slots = cells.shape[1]
    me = lax.axis_index("mem")
    after, before = neighbour_ids()
    peers = [lax.rem(me + p, parts) for p in range(1, parts)]
    targets = [after, before] + [{"mem": p} for p in peers]

    barrier = pltpu.get_barrier_semaphore()
    for target in targets:
        pl.semaphore_signal(barrier, inc=1, device_id=target, device_id_type=pl.DeviceIdType.MESH)
    for f in range(fields):
        for r in range(rows):
            row = members[f, :, r, :]
            first[width + r, f] = row
            if r >= rows - width:
                edges[0, f, r - (rows - width)] = row.astype(jnp.bfloat16)
            if r < width:
                edges[1, f, r] = row.astype(jnp.bfloat16)
    pl.semaphore_wait(barrier, len(targets))

    halo_copies = []
    for way, target in enumerate((after, before)):
        copy = pltpu.make_async_remote_copy(
            src_ref=edges.at[way],
            dst_ref=halo.at[way],
            send_sem=halo_send.at[way],
            recv_sem=halo_recv.at[way],
            device_id=target,
            device_id_type=pl.DeviceIdType.MESH,
        )
        copy.start()
        halo_copies.append(copy)

    buffers = (first, second)

    def run_rows(step, start, number):
        src, dst = buffers[step % 2], buffers[(step + 1) % 2]
        last = step == STEPS - 1

        def row_step(i, carry):
            row = i + start

            def at(which, m):
                return [src[which, f, pl.ds(m, 8), :] for f in range(fields)]

            for m in range(0, ens, 16):
                done = []
                for half in (m, m + 8):
                    done.append(advance(at(row - 1, half), at(row, half), at(row + 1, half)))
                    if not last:
                        for f in range(fields):
                            dst[row, f, pl.ds(half, 8), :] = done[-1][f]
                if last:
                    for f in range(fields):
                        both = jnp.concatenate([done[0][f], done[1][f]], axis=0)
                        both = both.astype(jnp.bfloat16)
                        for d in range(parts):
                            ready[d, f, row - width, pl.ds(m, 16), :] = both[:, d * tile_cols : (d + 1) * tile_cols]
            return carry

        lax.fori_loop(0, number, row_step, 0)

    for step in range(STEPS):
        inner = rows - 2 * (step + 1)
        if inner > 0:
            run_rows(step, width + step + 1, inner)
    chunk = 256 if points % 256 == 0 else tile_cols

    def select(i, carry):
        ids = lax.broadcasted_iota(jnp.int32, (chunk, slots), 0) + i * chunk
        start = pl.multiple_of(i * chunk, chunk)
        pick[pl.ds(start, chunk), :] = jnp.where(ids == cells[...], 1.0, 0.0).astype(jnp.bfloat16)
        return carry

    lax.fori_loop(0, points // chunk, select, 0)

    for copy in halo_copies:
        copy.wait_recv()
    for f in range(fields):
        for r in range(width):
            first[r, f] = halo[0, f, r].astype(jnp.float32)
            first[width + rows + r, f] = halo[1, f, r].astype(jnp.float32)

    sent = []

    def send(piece, f, row, number):
        group = []
        for p, peer in enumerate(peers):
            copy = pltpu.make_async_remote_copy(
                src_ref=ready.at[peer, f, pl.ds(row, number)],
                dst_ref=recv.at[me, f, pl.ds(row, number)],
                send_sem=part_send.at[piece, p],
                recv_sem=part_recv.at[piece, p],
                device_id={"mem": peer},
                device_id_type=pl.DeviceIdType.MESH,
            )
            copy.start()
            group.append(copy)
        sent.append(group)

    for step in range(STEPS - 1):
        edge = step + 1
        low_end = max(width + step + 1, edge)
        high_start = width + rows - (step + 1)
        if high_start > low_end:
            run_rows(step, edge, low_end - edge)
            run_rows(step, high_start, rows + 2 * width - edge - high_start)
        else:
            run_rows(step, edge, rows + 2 * width - 2 * edge)
    half_rows = rows // 2
    run_rows(STEPS - 1, width, half_rows)
    send(0, 0, 0, half_rows)
    run_rows(STEPS - 1, width + half_rows, rows - half_rows)
    send(1, 0, half_rows, rows - half_rows)
    for f in range(1, fields):
        send(f + 1, f, 0, rows)

    def place(f):
        recv[me, f] = ready[me, f]
        for s in range(parts):
            for r in range(rows):
                state[f, s * ens : (s + 1) * ens, r * tile_cols : (r + 1) * tile_cols] = recv[s, f, r]

    for group in sent[:2]:
        for copy in group:
            copy.wait_recv()
    place(0)
    observed = jnp.dot(state[0], pick[...], preferred_element_type=jnp.float32)
    mean = jnp.sum(observed, axis=0, keepdims=True) * (1.0 / full)
    spread = observed - mean
    std = error[...]
    slot_ids = lax.broadcasted_iota(jnp.int32, (1, slots), 1)
    weights = jnp.where(slot_ids < count[0, 0], 1.0 / (std * std), 0.0)
    weighted = spread * weights
    gram0 = lax.dot_general(
        weighted, spread, (((1,), (1,)), ((), ())), precision=HIGHEST, preferred_element_type=jnp.float32
    )
    rhs = jnp.dot(weighted * std, noise[...], precision=HIGHEST, preferred_element_type=jnp.float32)
    rhs = rhs + jnp.sum(weighted * (values[...] - mean), axis=1, keepdims=True) - gram0
    eye = jnp.where(
        lax.broadcasted_iota(jnp.int32, (full, full), 0) == lax.broadcasted_iota(jnp.int32, (full, full), 1), 1.0, 0.0
    )
    solved = eliminate(gram0 + (full - 1.0) * eye, rhs)
    centred = solved - jnp.sum(solved, axis=0, keepdims=True) * (1.0 / full) + eye
    turned = centred.T
    upper = turned.astype(jnp.bfloat16)
    lower = (turned - upper.astype(jnp.float32)).astype(jnp.bfloat16)
    for f in range(fields):
        if f > 0:
            for copy in sent[f + 1]:
                copy.wait_recv()
            place(f)
        for r in range(rows):
            block = state[f, :, r * tile_cols : (r + 1) * tile_cols]
            tall[:, r, :] = jnp.dot(upper, block, preferred_element_type=jnp.float32) + jnp.dot(
                lower, block, preferred_element_type=jnp.float32
            )
        out[f] = tall[...].astype(jnp.bfloat16)
    for copy in halo_copies:
        copy.wait_send()
    for group in sent:
        for copy in group:
            copy.wait_send()


def vmem():
    return pl.BlockSpec(memory_space=pltpu.VMEM)


def body(members, obs_cells, obs_count, obs_values, obs_error, obs_noise):
    fields, ens, rows, cols = members.shape
    parts = lax.axis_size("mem")
    tile_cols = cols // parts
    full = ens * parts
    points = rows * tile_cols
    slots = obs_cells.shape[2]
    pieces = fields + 1
    shared = pltpu.VMEM((rows + 2 * STEPS, fields, ens, cols), jnp.float32)
    edge = pltpu.VMEM((2, fields, STEPS, ens, cols), jnp.bfloat16)
    part = pltpu.VMEM((parts, fields, rows, ens, tile_cols), jnp.bfloat16)
    return pl.pallas_call(
        kernel,
        name="assimilate",
        out_shape=jax.ShapeDtypeStruct((fields, full, rows, tile_cols), jnp.bfloat16),
        in_specs=[vmem(), pl.BlockSpec(memory_space=pltpu.SMEM)] + [vmem()] * 4,
        out_specs=vmem(),
        scratch_shapes=[
            shared,
            shared,
            edge,
            edge,
            part,
            part,
            pltpu.VMEM((fields, full, points), jnp.bfloat16),
            pltpu.VMEM((points, slots), jnp.bfloat16),
            pltpu.VMEM((full, rows, tile_cols), jnp.float32),
            pltpu.SemaphoreType.DMA((2,)),
            pltpu.SemaphoreType.DMA((2,)),
            pltpu.SemaphoreType.DMA((pieces, parts - 1)),
            pltpu.SemaphoreType.DMA((pieces, parts - 1)),
        ],
        compiler_params=pltpu.CompilerParams(
            vmem_limit_bytes=VMEM_BYTES, collective_id=0, has_side_effects=True
        ),
    )(members, obs_count, obs_cells[0], obs_values[0], obs_error[0], obs_noise[0, 0])


def solution(mesh):
    in_specs = (
        P(None, "mem", ("tile", "grp"), None),
        P(("tile", "grp"), "mem", None),
        P(("tile", "grp"), "mem"),
        P(("tile", "grp"), "mem", None),
        P(("tile", "grp"), "mem", None),
        P(("tile", "grp"), "mem", None, None),
    )
    out_specs = P(None, None, ("tile", "grp"), "mem")
    return jax.shard_map(body, mesh=mesh, in_specs=in_specs, out_specs=out_specs, check_vma=False)
```

time: 56 us -> 48.5 us (0.87)
  waiting for transfers between devices: 18.4 us -> 0 us
  Pallas kernels: 25.3 us -> 42.2 us
  starting transfers between devices: 9.05 us -> 0 us
  local copies, waits for them, and re-layouts: 2.44 us -> 5.38 us
    pallas_call x2 -> x1, Pallas kernels: 25.3 us -> 42.2 us  [body(): pl.pallas_call(kernel, name='assimilate', out_shape=jax.ShapeDtypeStruct(...]
    all_to_all x1 -> x0, waiting for transfers between devices: 10.9 us -> none  [body(): recv = lax.all_to_all(ready, 'mem', split_axis=0, concat_axis=0)]
    ppermute x2 -> x0, waiting for transfers between devices: 7.45 us -> none  [the longest x1 7.01 us: body(): low = lax.ppermute(edge(members[:, :, rows - STEPS:, :]), axes, forward)]
    ppermute x2 -> x0, starting transfers between devices: 4.64 us -> none  [the longest x1 4.09 us: body(): high = lax.ppermute(edge(members[:, :, :STEPS, :]), axes, backward)]
    all_to_all x1 -> x0, starting transfers between devices: 4.42 us -> none  [body(): recv = lax.all_to_all(ready, 'mem', split_axis=0, concat_axis=0)]
    unnamed x11, local copies, waits for them, and re-layouts: 2.39 us -> 5.38 us
  transfers between devices with their start and end apart: 3 -> 0, of which waited for: 3 -> 0; matrix products, arithmetic and copies ran while one was open for 0% -> 0% of each run, Pallas kernels for 0% -> 0%
where the time goes in v2:
time: 48.5 us; the launch traced here: 48.2 us
  Pallas kernels  42.2 us (87%)
  local copies, waits for them, and re-layouts  5.38 us (11%)
  between operations  0.67 us (1%)
    pallas_call x1, Pallas kernels, body(): pl.pallas_call(kernel, name='assimilate', out_shape=jax.ShapeDtypeStruct(...  42.2 us
    unnamed x11, local copies, waits for them, and re-layouts  5.38 us

profile of v2, /device:TPU:0, one launch (start us, length us, event | category | flops | bytes accessed | tf_op | source)
XLA Modules:
  0.0 48.2 jit_solution(6941498477227657826)
XLA Ops:
  0.7 0.0 copy-start
  0.7 1.4 %copy-done = f32[3,32,8,512]{3,2,1,0:T(8,128)S(1)} copy-done((f32[3,32,8,512]{3,2,1,0:T(8,128)S(1)}, f32[3,32,8,512]{3,2,1,0:T(8,128)}, u32[]{:S(2)}) %copy-start) | copy-done | bytes 1572888
  2.1 0.0 copy-start.1
  2.1 1.0 %copy-done.1 = f32[1,1,1024,128]{3,2,1,0:T(8,128)S(1)} copy-done((f32[1,1,1024,128]{3,2,1,0:T(8,128)S(1)}, f32[1,1,1024,128]{3,2,1,0:T(8,128)}, u32[]{:S(2)}) %copy-start.1) | copy-done | bytes 524312
  3.1 0.0 copy-start.2
  3.1 0.7 %copy-done.2 = s32[1,1,1024]{2,1,0:T(1,128)S(1)} copy-done((s32[1,1,1024]{2,1,0:T(1,128)S(1)}, s32[1,1,1024]{2,1,0:T(1,128)}, u32[]{:S(2)}) %copy-start.2) | copy-done | bytes 4120
  3.8 0.0 copy-start.3
  3.8 0.7 %copy-done.3 = f32[1,1,1024]{2,1,0:T(1,128)S(1)} copy-done((f32[1,1,1024]{2,1,0:T(1,128)S(1)}, f32[1,1,1024]{2,1,0:T(1,128)}, u32[]{:S(2)}) %copy-start.3) | copy-done | bytes 4120
  4.5 0.0 copy-start.4
  4.5 0.7 %copy-done.4 = f32[1,1,1024]{2,1,0:T(1,128)S(1)} copy-done((f32[1,1,1024]{2,1,0:T(1,128)S(1)}, f32[1,1,1024]{2,1,0:T(1,128)}, u32[]{:S(2)}) %copy-start.4) | copy-done | bytes 4120
  5.2 42.2 %assimilate.1 = bf16[3,128,8,128]{3,2,1,0:T(8,128)(2,1)S(1)} custom-call(f32[3,32,8,512]{3,2,1,0:T(8,128)S(1)} %copy-done, s32[1,1]{1,0:T(1,128)S(6)} %copy.8.count, s32[1,1024]{1,0:T(1,128)S(1)} %bitcast.5, f32[1,1024]{1,0:T(1,128)S(1)} %bitcast.6, f32[1,1024]{1,0:T(1,128)S(1)} %bitcast.7, f32[1024,128]{1,0:T(8,128)S(1)} %bitcast.4), custom_call_target="tpu_custom_call" | custom-call | tf_op jit(solution)/shard_map/assimilate/pallas_call | solution.py:261
  47.3 0.9 %copy.9 = bf16[3,128,8,128]{3,2,1,0:T(8,128)(2,1)} copy(bf16[3,128,8,128]{3,2,1,0:T(8,128)(2,1)S(1)} %assimilate.1) | data formatting | bytes 1572864
Async XLA Ops:
  0.7 1.4 %copy-start = (f32[3,32,8,512]{3,2,1,0:T(8,128)S(1)}, f32[3,32,8,512]{3,2,1,0:T(8,128)}, u32[]{:S(2)}) copy-start(f32[3,32,8,512]{3,2,1,0:T(8,128)} %members.1) | copy-start | bytes 4718596
  2.1 1.0 %copy-start.1 = (f32[1,1,1024,128]{3,2,1,0:T(8,128)S(1)}, f32[1,1,1024,128]{3,2,1,0:T(8,128)}, u32[]{:S(2)}) copy-start(f32[1,1,1024,128]{3,2,1,0:T(8,128)} %param.11) | copy-start | bytes 1572868
  3.1 0.7 %copy-start.2 = (s32[1,1,1024]{2,1,0:T(1,128)S(1)}, s32[1,1,1024]{2,1,0:T(1,128)}, u32[]{:S(2)}) copy-start(s32[1,1,1024]{2,1,0:T(1,128)} %param.7) | copy-start | bytes 12292
  3.8 0.7 %copy-start.3 = (f32[1,1,1024]{2,1,0:T(1,128)S(1)}, f32[1,1,1024]{2,1,0:T(1,128)}, u32[]{:S(2)}) copy-start(f32[1,1,1024]{2,1,0:T(1,128)} %param.9) | copy-start | bytes 12292
  4.5 0.7 %copy-start.4 = (f32[1,1,1024]{2,1,0:T(1,128)S(1)}, f32[1,1,1024]{2,1,0:T(1,128)}, u32[]{:S(2)}) copy-start(f32[1,1,1024]{2,1,0:T(1,128)} %param.10) | copy-start | bytes 12292
